TPU v7x, 256 devices: a whole 4x4x8 slice. The times are simulated.
256 devices in a mesh: layer: 8 (over z), latent: 32 (over x, y, core).
Axes of the slice: x: 4, y: 4, z: 8, core: 2. Of those that a mesh axis runs over, the one named last changes fastest.
Arguments:
- resid: bfloat16 [8, 1024, 4096], P('layer', 'latent'), may hold values from -6 to 6
- mlp_out: bfloat16 [8, 1024, 4096], P('layer', 'latent'), may hold values from -6 to 6
- enc_w: bfloat16 [8, 4096, 4096], P('layer', None, 'latent'), may hold values from -0.09375 to 0.09375
- enc_b: float32 [8, 4096], P('layer', 'latent'), may hold values from -3 to 3
- dec_w: bfloat16 [8, 8, 4096, 4096], P('layer', None, 'latent'), may hold values from -0.03125 to 0.03125
Outputs:
- error: bfloat16 [8, 1024, 4096], P('layer', 'latent')
All inputs are finite; a program needn't handle non-finite values.
Results may differ from a plain program's by a relative error of at most 0.0034.
Values may be sent and summed in bfloat16 or wider, within the bound.
A program may use at most 128 MiB of HBM per device.

v0:
```python
import jax
import jax.numpy as jnp
from jax import lax
from jax.sharding import PartitionSpec as P


def body(resid, mlp_out, enc_w, enc_b, dec_w):
    target = lax.axis_index("layer")
    weights = dec_w[0]
    encoder = enc_w[0]
    bias = enc_b[0]
    pre = (
        jnp.dot(
            lax.all_gather(resid[0], "latent", axis=0, tiled=True),
            encoder,
            preferred_element_type=jnp.float32,
        )
        + bias
    )
    own_latents = jnp.maximum(pre, 0.0).astype(jnp.bfloat16)
    empty = jnp.zeros((own_latents.shape[0], weights.shape[2]), jnp.float32)
    recon = empty
    pieces = lax.all_gather(own_latents[None], "layer", axis=0, tiled=True)
    start = jnp.int32(0)
    for offset in range(pieces.shape[0]):
        block = pieces[offset]
        source = start + offset

        def added(value):
            chosen = lax.dynamic_index_in_dim(weights, source, 0, keepdims=False)
            return value + jnp.dot(block, chosen, preferred_element_type=jnp.float32)

        recon = lax.cond(
            jnp.logical_and(source >= 0, source <= target), added, lambda value: value, recon
        )
    mine = lax.psum_scatter(recon, "latent", scatter_dimension=0, tiled=True)
    return (mlp_out[0].astype(jnp.float32) - mine).astype(jnp.bfloat16)[None]


def solution(mesh):
    return jax.shard_map(
        body,
        mesh=mesh,
        in_specs=(
            P("layer", "latent", None),
            P("layer", "latent", None),
            P("layer", None, "latent"),
            P("layer", "latent"),
            P("layer", None, "latent", None),
        ),
        out_specs=P("layer", "latent", None),
        check_vma=False,
    )
```

profile of v0, /device:TPU:224, one launch (start us, length us, event | category | flops | bytes accessed | tf_op | source)
XLA Modules:
  0.0 353.6 jit_solution(1592630393347481117)
XLA Ops:
  6.5 0.7 all-gather.5.cloned.1.call-update
  7.3 0.0 all-gather.7.cloned.1.call-start
  7.3 60.8 %all-gather.5.cloned.1.call-done = bf16[1,1024,4096]{2,1,0:T(8,128)(2,1)} async-done(((bf16[1,32,4096]{2,1,0:T(8,128)(2,1)}), bf16[1,1024,4096]{2,1,0:T(8,128)(2,1)}) %all-gather.5.cloned.1.call-update) | async-done | bytes 8388624 | tf_op jit(solution)/shard_map/all_gather | solution.py:14
  68.1 6.4 %fusion.41 = bf16[1024,128]{1,0:T(8,128)(2,1)} fusion(bf16[1,1024,4096]{2,1,0:T(8,128)(2,1)} %all-gather.5.cloned.1.call-done, bf16[1,4096,128]{2,1,0:T(8,128)(2,1)S(1)} %copy-done, f32[128]{0:T(128)} %bitcast.84), kind=kOutput, calls=%fused_computation.44 | convolution fusion | flops 1074135040 | bytes 9699840 | tf_op jit(solution)/shard_map/dot_general | solution.py:13
  74.6 0.0 reduce-scatter.2.cloned.1.call-start
  74.7 39.4 %all-gather.7.cloned.1.call-done = bf16[8192,128]{1,0:T(8,128)(2,1)} async-done(((bf16[1024,128]{1,0:T(8,128)(2,1)}), bf16[8192,128]{1,0:T(8,128)(2,1)}) %all-gather.7.cloned.1.call-update) | async-done | bytes 2097168 | tf_op jit(solution)/shard_map/all_gather | solution.py:23
  114.0 9.4 %conditional.8 = (f32[1024,4096]{1,0:T(8,128)}) conditional(s32[]{:T(128)} %convert_element_type.45, () %tuple.53, (bf16[8,128,4096]{2,1,0:T(8,128)(2,1)}, bf16[8,1024,128]{2,1,0:T(8,128)(2,1)}) %tuple.92), branch_computations={%region_0.0_spmd, %region_1.2_spmd} | conditional | flops 1073741824 | bytes 18087944 | solution.py:33
  114.0 9.4 %fusion = f32[1024,4096]{1,0:T(8,128)} fusion(bf16[8,128,4096]{2,1,0:T(8,128)(2,1)} %get-tuple-element.85, bf16[8,1024,128]{2,1,0:T(8,128)(2,1)} %get-tuple-element.108), kind=kOutput, calls=%fused_computation | convolution fusion | flops 1073741824 | bytes 18087936 | tf_op jit(solution)/shard_map/cond/branch_1_fun/dot_general | solution.py:31
  123.4 14.2 %conditional.9 = (f32[1024,4096]{1,0:T(8,128)}) conditional(s32[]{:T(128)} %convert_element_type.44, f32[1024,4096]{1,0:T(8,128)} %get-tuple-element.121, (bf16[8,128,4096]{2,1,0:T(8,128)(2,1)}, bf16[8,1024,128]{2,1,0:T(8,128)(2,1)}, f32[1024,4096]{1,0:T(8,128)}) %tuple.93), branch_computations={%region_2.3_spmd, %region_3.4_spmd} | conditional | flops 1077936128 | bytes 34865160 | solution.py:33
  123.4 14.2 %convolution_add_fusion = f32[1024,4096]{1,0:T(8,128)} fusion(f32[1024,4096]{1,0:T(8,128)} %get-tuple-element.86, bf16[8,128,4096]{2,1,0:T(8,128)(2,1)} %get-tuple-element.88, bf16[8,1024,128]{2,1,0:T(8,128)(2,1)} %get-tuple-element.110), kind=kOutput, calls=%fused_computation.5 | convolution fusion | flops 1077936128 | bytes 34865152 | tf_op jit(solution)/shard_map/cond/branch_1_fun/dot_general | solution.py:31
  137.6 14.2 %conditional.10 = (f32[1024,4096]{1,0:T(8,128)}) conditional(s32[]{:T(128)} %convert_element_type.43, f32[1024,4096]{1,0:T(8,128)} %get-tuple-element.122, (bf16[8,128,4096]{2,1,0:T(8,128)(2,1)}, bf16[8,1024,128]{2,1,0:T(8,128)(2,1)}, f32[1024,4096]{1,0:T(8,128)}) %tuple.94), branch_computations={%region_4.5_spmd, %region_5.6_spmd} | conditional | flops 1077936128 | bytes 34865160 | solution.py:33
  137.6 14.2 %convolution_add_fusion.1 = f32[1024,4096]{1,0:T(8,128)} fusion(f32[1024,4096]{1,0:T(8,128)} %get-tuple-element.89, bf16[8,128,4096]{2,1,0:T(8,128)(2,1)} %get-tuple-element.91, bf16[8,1024,128]{2,1,0:T(8,128)(2,1)} %get-tuple-element.112), kind=kOutput, calls=%fused_computation.10 | convolution fusion | flops 1077936128 | bytes 34865152 | tf_op jit(solution)/shard_map/cond/branch_1_fun/dot_general | solution.py:31
  151.9 14.2 %conditional.11 = (f32[1024,4096]{1,0:T(8,128)}) conditional(s32[]{:T(128)} %convert_element_type.42, f32[1024,4096]{1,0:T(8,128)} %get-tuple-element.123, (bf16[8,128,4096]{2,1,0:T(8,128)(2,1)}, bf16[8,1024,128]{2,1,0:T(8,128)(2,1)}, f32[1024,4096]{1,0:T(8,128)}) %tuple.95), branch_computations={%region_6.7_spmd, %region_7.8_spmd} | conditional | flops 1077936128 | bytes 34865160 | solution.py:33
  151.9 14.2 %convolution_add_fusion.2 = f32[1024,4096]{1,0:T(8,128)} fusion(f32[1024,4096]{1,0:T(8,128)} %get-tuple-element.92, bf16[8,128,4096]{2,1,0:T(8,128)(2,1)} %get-tuple-element.94, bf16[8,1024,128]{2,1,0:T(8,128)(2,1)} %get-tuple-element.114), kind=kOutput, calls=%fused_computation.15 | convolution fusion | flops 1077936128 | bytes 34865152 | tf_op jit(solution)/shard_map/cond/branch_1_fun/dot_general | solution.py:31
  166.1 14.2 %conditional.12 = (f32[1024,4096]{1,0:T(8,128)}) conditional(s32[]{:T(128)} %convert_element_type.41, f32[1024,4096]{1,0:T(8,128)} %get-tuple-element.124, (bf16[8,128,4096]{2,1,0:T(8,128)(2,1)}, bf16[8,1024,128]{2,1,0:T(8,128)(2,1)}, f32[1024,4096]{1,0:T(8,128)}) %tuple.96), branch_computations={%region_8.9_spmd, %region_9.10_spmd} | conditional | flops 1077936128 | bytes 34865160 | solution.py:33
  166.1 14.2 %convolution_add_fusion.3 = f32[1024,4096]{1,0:T(8,128)} fusion(f32[1024,4096]{1,0:T(8,128)} %get-tuple-element.95, bf16[8,128,4096]{2,1,0:T(8,128)(2,1)} %get-tuple-element.97, bf16[8,1024,128]{2,1,0:T(8,128)(2,1)} %get-tuple-element.116), kind=kOutput, calls=%fused_computation.20 | convolution fusion | flops 1077936128 | bytes 34865152 | tf_op jit(solution)/shard_map/cond/branch_1_fun/dot_general | solution.py:31
  180.4 14.2 %conditional.13 = (f32[1024,4096]{1,0:T(8,128)}) conditional(s32[]{:T(128)} %convert_element_type.40, f32[1024,4096]{1,0:T(8,128)} %get-tuple-element.125, (bf16[8,128,4096]{2,1,0:T(8,128)(2,1)}, bf16[8,1024,128]{2,1,0:T(8,128)(2,1)}, f32[1024,4096]{1,0:T(8,128)}) %tuple.97), branch_computations={%region_10.11_spmd, %region_11.12_spmd} | conditional | flops 1077936128 | bytes 34865160 | solution.py:33
  180.4 14.2 %convolution_add_fusion.4 = f32[1024,4096]{1,0:T(8,128)} fusion(f32[1024,4096]{1,0:T(8,128)} %get-tuple-element.98, bf16[8,128,4096]{2,1,0:T(8,128)(2,1)} %get-tuple-element.100, bf16[8,1024,128]{2,1,0:T(8,128)(2,1)} %get-tuple-element.118), kind=kOutput, calls=%fused_computation.25 | convolution fusion | flops 1077936128 | bytes 34865152 | tf_op jit(solution)/shard_map/cond/branch_1_fun/dot_general | solution.py:31
  194.6 14.2 %conditional.14 = (f32[1024,4096]{1,0:T(8,128)}) conditional(s32[]{:T(128)} %convert_element_type.39, f32[1024,4096]{1,0:T(8,128)} %get-tuple-element.126, (bf16[8,128,4096]{2,1,0:T(8,128)(2,1)}, bf16[8,1024,128]{2,1,0:T(8,128)(2,1)}, f32[1024,4096]{1,0:T(8,128)}) %tuple.98), branch_computations={%region_12.13_spmd, %region_13.14_spmd} | conditional | flops 1077936128 | bytes 34865160 | solution.py:33
  194.6 14.2 %convolution_add_fusion.5 = f32[1024,4096]{1,0:T(8,128)} fusion(f32[1024,4096]{1,0:T(8,128)} %get-tuple-element.101, bf16[8,128,4096]{2,1,0:T(8,128)(2,1)} %get-tuple-element.103, bf16[8,1024,128]{2,1,0:T(8,128)(2,1)} %get-tuple-element.120), kind=kOutput, calls=%fused_computation.30 | convolution fusion | flops 1077936128 | bytes 34865152 | tf_op jit(solution)/shard_map/cond/branch_1_fun/dot_general | solution.py:31
  208.9 14.2 %conditional.15 = (f32[1024,4096]{1,0:T(8,128)}) conditional(s32[]{:T(128)} %convert_element_type.38, f32[1024,4096]{1,0:T(8,128)} %get-tuple-element.127, (bf16[8,1024,128]{2,1,0:T(8,128)(2,1)}, bf16[8,128,4096]{2,1,0:T(8,128)(2,1)}, f32[1024,4096]{1,0:T(8,128)}) %tuple.99), branch_computations={%region_14.15_spmd, %region_15.16_spmd} | conditional | flops 1077936128 | bytes 34865160 | solution.py:33
  208.9 14.2 %convolution_add_fusion.6 = f32[1024,4096]{1,0:T(8,128)} fusion(f32[1024,4096]{1,0:T(8,128)} %get-tuple-element.104, bf16[8,128,4096]{2,1,0:T(8,128)(2,1)} %get-tuple-element.106, bf16[8,1024,128]{2,1,0:T(8,128)(2,1)} %get-tuple-element.105), kind=kOutput, calls=%fused_computation.35 | convolution fusion | flops 1077936128 | bytes 34865152 | tf_op jit(solution)/shard_map/cond/branch_1_fun/dot_general | solution.py:31
  223.1 122.1 %reduce-scatter.2.cloned.1.call-done = f32[32,4096]{1,0:T(8,128)} async-done(((f32[1024,4096]{1,0:T(8,128)}), f32[32,4096]{1,0:T(8,128)}) %reduce-scatter.2.cloned.1.call-update) | async-done | bytes 524304 | tf_op jit(solution)/shard_map/reduce_scatter | solution.py:36
  345.2 1.8 fusion.46
  (7 shorter events, 0.0 us)
Async XLA Ops:
  6.5 61.6 %copy-start = (bf16[1,4096,128]{2,1,0:T(8,128)(2,1)S(1)}, bf16[1,4096,128]{2,1,0:T(8,128)(2,1)}, u32[]{:S(2)}) copy-start(bf16[1,4096,128]{2,1,0:T(8,128)(2,1)} %param.23) | copy-start | bytes 3145732
  6.5 61.6 %all-gather.5.cloned.1.call-start = ((), (), s32[]{:S(2)}) async-start(), calls=%async_computation.2 | async-start | bytes 8650752 | tf_op jit(solution)/shard_map/all_gather | solution.py:14
  7.3 106.8 %all-gather.7.cloned.1.call-start = ((), (), s32[]{:S(2)}) async-start(), calls=%async_computation.3 | async-start | bytes 2359296 | tf_op jit(solution)/shard_map/all_gather | solution.py:23
  74.6 270.6 %reduce-scatter.2.cloned.1.call-start = ((), (), s32[]{:S(2)}) async-start(), calls=%async_computation.1 | async-start | bytes 17301504 | tf_op jit(solution)/shard_map/reduce_scatter | solution.py:36
  223.1 122.1 %copy-start.1 = (bf16[1,32,4096]{2,1,0:T(8,128)(2,1)S(1)}, bf16[1,32,4096]{2,1,0:T(8,128)(2,1)}, u32[]{:S(2)}) copy-start(bf16[1,32,4096]{2,1,0:T(8,128)(2,1)} %param.22) | copy-start | bytes 786436
Sparse Core Ops, SparseCore 0:
  9.9 58.1 all-gather.4
  74.7 39.2 all-gather.6
  223.3 121.9 reduce-scatter.1
where the time goes:
time: 356 us; the launch traced here: 354 us
  waiting for transfers between devices  223 us (63%)
  matrix products  116 us (33%)
  between operations  13.1 us (4%)
    reduce_scatter x1, waiting for transfers between devices, body(): mine = lax.psum_scatter(recon, 'latent', scatter_dimension=0, tiled=True)  122 us
    dot_general x8, matrix products, added(): return value + jnp.dot(block, chosen, preferred_element_type=jnp.float32)  109 us
    all_gather x1, waiting for transfers between devices, body(): lax.all_gather(resid[0], 'latent', axis=0, tiled=True)  60.8 us
    all_gather x1, waiting for transfers between devices, body(): pieces = lax.all_gather(own_latents[None], 'layer', axis=0, tiled=True)  39.4 us
  transfers between devices with their start and end apart: 3, of which 3 were waited for; matrix products, arithmetic and copies ran while one was open for 0% of the time, Pallas kernels for 0%

commit v1 on v0

v1 whole, which is shorter than its diff:
```python
import functools

import jax
import jax.numpy as jnp
from jax import lax
from jax.experimental import pallas as pl
from jax.experimental.pallas import tpu as pltpu
from jax.sharding import PartitionSpec as P

MESH = pl.DeviceIdType.MESH
LAYERS = 8
SIDE = 4
CHUNKS = 2
ROWS = 16
D = 4096
HALF = 2048
QUARTER = 1024
LANES = 128
TILE = 512
OFFSETS = (1, SIDE - 1, 2)
FORWARD = 4
BACKWARD = 3


def kernel(
    resid, mlp, enc, bias, dec, out,
    R, WE, BE, WD, L, ACC, S, TA, TB, VA, VB, UA, UB, MV, OV,
    ag1_s, ag1_r, ag2_s, ag2_r, w_s, w_r, d_s, d_r, zf_s, zf_r, zb_s, zb_r,
    rs1_s, rs1_r, rs2_s, rs2_r, own_sem, loc_sem, dloc_sem, out_sem,
):
    z = lax.axis_index("layer")
    index = lax.axis_index("latent")
    core = lax.rem(index, 2)
    y = lax.rem(lax.div(index, 2), SIDE)
    x = lax.div(index, 2 * SIDE)

    def at_chip(px, py):
        return {"layer": z, "latent": (px * SIDE + py) * 2 + core}

    def at_layer(pz):
        return {"layer": pz, "latent": index}

    partner = {"layer": z, "latent": index + 1 - 2 * core}

    def move(v, o):
        return lax.rem(v + o, SIDE)

    def remote(src, dst, ss, rs, where):
        return pltpu.make_async_remote_copy(
            src_ref=src, dst_ref=dst, send_sem=ss, recv_sem=rs,
            device_id=where, device_id_type=MESH,
        )

    up, down = lax.rem(z + 1, LAYERS), lax.rem(z + LAYERS - 1, LAYERS)

    barrier = pltpu.get_barrier_semaphore()
    friends = [partner, at_layer(up), at_layer(down)]
    friends += [at_chip(move(x, o), y) for o in OFFSETS]
    friends += [at_chip(x, move(y, o)) for o in OFFSETS]
    for friend in friends:
        pl.semaphore_signal(barrier, inc=1, device_id=friend, device_id_type=MESH)
    pl.semaphore_wait(barrier, len(friends))

    def ag1(q, h, j):
        cols = pl.ds(h * HALF, HALF)
        o = OFFSETS[j]
        where = at_chip(move(x, o), y) if h == 0 else at_chip(x, move(y, o))
        return remote(
            resid.at[0, pl.ds(q * ROWS, ROWS), cols], R.at[q, x, y, :, cols],
            ag1_s.at[q, h, j], ag1_r.at[q, h, j], where,
        )

    def ag1_start(q):
        for j in range(3):
            for h in range(2):
                ag1(q, h, j).start()

    def ag1_wait(q, h):
        cols = pl.ds(h * HALF, HALF)
        for j in range(3):
            back = SIDE - OFFSETS[j]
            slot = R.at[q, move(x, back), y, :, cols] if h == 0 else R.at[q, x, move(y, back), :, cols]
            remote(slot, slot, ag1_s.at[q, h, j], ag1_r.at[q, h, j], partner).wait_recv()

    def lines(q, h, back, cols):
        if h == 0:
            return R.at[q, :, move(y, back), :, cols]
        return R.at[q, move(x, back), :, :, cols]

    def ag2(q, h, direction, piece):
        step = 1 if direction == 0 else SIDE - 1
        first = direction if piece != 1 else 1 - direction
        cols = pl.ds(h * HALF + first * QUARTER, QUARTER)
        back = 0 if piece < 2 else SIDE - step
        where = at_chip(x, move(y, step)) if h == 0 else at_chip(move(x, step), y)
        block = lines(q, h, back, cols)
        return remote(block, block, ag2_s.at[q, h, direction, piece], ag2_r.at[q, h, direction, piece], where)

    def ag2_arrive(q, h, direction, piece):
        step = 1 if direction == 0 else SIDE - 1
        first = direction if piece != 1 else 1 - direction
        cols = pl.ds(h * HALF + first * QUARTER, QUARTER)
        back = SIDE - step if piece < 2 else 2
        block = lines(q, h, back, cols)
        remote(block, block, ag2_s.at[q, h, direction, piece], ag2_r.at[q, h, direction, piece], partner).wait_recv()

    def ag2_start(q, h):
        for piece in range(2):
            for direction in range(2):
                ag2(q, h, direction, piece).start()

    def ag2_relay(q):
        for h in range(2):
            for direction in range(2):
                ag2_arrive(q, h, direction, 0)
                ag2(q, h, direction, 2).start()

    def ag2_rest(q):
        for piece in (1, 2):
            for h in range(2):
                for direction in range(2):
                    ag2_arrive(q, h, direction, piece)

    mine = pl.ds(pl.multiple_of(core * LANES, LANES), LANES)
    theirs = pl.ds(pl.multiple_of(LANES - core * LANES, LANES), LANES)

    def enc_pair():
        return (
            remote(enc.at[0], WE.at[:, mine], w_s.at[0], w_r.at[0], partner),
            remote(bias, BE.at[:, mine], w_s.at[1], w_r.at[1], partner),
        )

    def enc_local():
        return (
            pltpu.make_async_copy(enc.at[0], WE.at[:, mine], loc_sem.at[0]),
            pltpu.make_async_copy(bias, BE.at[:, mine], loc_sem.at[1]),
        )

    def dec_remote(s):
        return remote(dec.at[0, s], WD.at[s, mine, :], d_s.at[s], d_r.at[s], partner)

    def dec_arrive(s):
        slot = WD.at[s, theirs, :]
        remote(slot, slot, d_s.at[s], d_r.at[s], partner).wait_recv()

    def dec_local(s):
        return pltpu.make_async_copy(dec.at[0, s], WD.at[s, mine, :], dloc_sem.at[s])

    def own_rows(q):
        return pltpu.make_async_copy(resid.at[0, pl.ds(q * ROWS, ROWS), :], R.at[q, x, y], own_sem.at[q])

    mlp_copy = pltpu.make_async_copy(mlp.at[0], MV, loc_sem.at[2])

    def encode(q):
        if q == 0:
            for copy in enc_local():
                copy.wait()
            for slot, k in ((WE.at[:, theirs], 0), (BE.at[:, theirs], 1)):
                remote(slot, slot, w_s.at[k], w_r.at[k], partner).wait_recv()
        rows = R[q].reshape(SIDE * SIDE * ROWS, D)
        pre = jnp.dot(rows, WE[...], preferred_element_type=jnp.float32) + BE[...]
        L[q, z] = jnp.maximum(pre, 0.0).astype(jnp.bfloat16)

    def z_forward(q, i):
        s = lax.rem(z + LAYERS - i, LAYERS)
        return remote(L.at[q, s], L.at[q, s], zf_s.at[q, i], zf_r.at[q, i], at_layer(up))

    def forward_sends(i):
        return jnp.logical_and(z >= i, z < LAYERS - 1)

    def z_backward(q, i):
        s = lax.rem(z + i, LAYERS)
        return remote(L.at[q, s], L.at[q, s], zb_s.at[q, i], zb_r.at[q, i], at_layer(down))

    def backward_sends(i):
        return lax.rem(z + i, LAYERS) < BACKWARD

    def z_send(q, i):
        if i < FORWARD:
            @pl.when(forward_sends(i))
            def _():
                z_forward(q, i).start()
        if i < BACKWARD:
            @pl.when(backward_sends(i))
            def _():
                z_backward(q, i).start()

    def z_arrive(q, i):
        if i < FORWARD:
            @pl.when(z >= i + 1)
            def _():
                slot = L.at[q, lax.rem(z + LAYERS - 1 - i, LAYERS)]
                remote(slot, slot, zf_s.at[q, i], zf_r.at[q, i], partner).wait_recv()
        if i < BACKWARD:
            @pl.when(lax.rem(z + 1 + i, LAYERS) < BACKWARD)
            def _():
                slot = L.at[q, lax.rem(z + 1 + i, LAYERS)]
                remote(slot, slot, zb_s.at[q, i], zb_r.at[q, i], partner).wait_recv()

    def add(q, s, first):
        def tile(n, carry):
            cols = pl.ds(pl.multiple_of(n * TILE, TILE), TILE)
            part = jnp.dot(L[q, s], WD[s, :, cols], preferred_element_type=jnp.float32)
            part = part.reshape(SIDE, SIDE, ROWS, TILE)
            if first:
                ACC[q, :, :, :, cols] = part
            else:
                ACC[q, :, :, :, cols] += part
            return carry

        lax.fori_loop(0, D // TILE, tile, 0)

    def z_add(q, i):
        if i < FORWARD:
            @pl.when(z >= i + 1)
            def _():
                add(q, lax.rem(z + LAYERS - 1 - i, LAYERS), False)
        if i < BACKWARD:
            source = lax.rem(z + 1 + i, LAYERS)

            @pl.when(jnp.logical_and(source < BACKWARD, source < z))
            def _():
                add(q, source, False)

    def z_step(q, i):
        z_arrive(q, i)
        z_send(q, i + 1)
        z_add(q, i)

    def rs1(q, h, j):
        cols = pl.ds(h * HALF, HALF)
        o = OFFSETS[j]
        if h == 0:
            return remote(S.at[q, move(x, o), :, :, cols], TA.at[q, j], rs1_s.at[q, h, j], rs1_r.at[q, h, j], at_chip(move(x, o), y))
        return remote(S.at[q, :, move(y, o), :, cols], TB.at[q, j], rs1_s.at[q, h, j], rs1_r.at[q, h, j], at_chip(x, move(y, o)))

    def rs1_start(q):
        def tile(n, carry):
            cols = pl.ds(pl.multiple_of(n * TILE, TILE), TILE)
            S[q, :, :, :, cols] = ACC[q, :, :, :, cols].astype(jnp.bfloat16)
            return carry

        lax.fori_loop(0, D // TILE, tile, 0)
        for j in (2, 0, 1):
            for h in range(2):
                rs1(q, h, j).start()

    def rs2(q, h, j):
        o = OFFSETS[j]
        if h == 0:
            return remote(VA.at[q, move(y, o)], UA.at[q, j], rs2_s.at[q, h, j], rs2_r.at[q, h, j], at_chip(x, move(y, o)))
        return remote(VB.at[q, move(x, o)], UB.at[q, j], rs2_s.at[q, h, j], rs2_r.at[q, h, j], at_chip(move(x, o), y))

    def rs2_start(q):
        for h, T, V in ((0, TA, VA), (1, TB, VB)):
            cols = pl.ds(h * HALF, HALF)
            for j in (0, 1, 2):
                slot = T.at[q, j]
                remote(slot, slot, rs1_s.at[q, h, j], rs1_r.at[q, h, j], partner).wait_recv()

            def line(k, carry):
                at = (q, x, k, slice(None), cols) if h == 0 else (q, k, y, slice(None), cols)
                total = ACC[at]
                for j in range(3):
                    total = total + T[q, j, k].astype(jnp.float32)
                ACC[at] = total
                V[q, k] = total.astype(jnp.bfloat16)
                return carry

            lax.fori_loop(0, SIDE, line, 0)
            for j in (2, 0, 1):
                rs2(q, h, j).start()

    def finish(q):
        if q == 0:
            mlp_copy.wait()
        rows = pl.ds(q * ROWS, ROWS)
        for h, U in ((0, UA), (1, UB)):
            cols = pl.ds(h * HALF, HALF)
            for j in (0, 1, 2):
                slot = U.at[q, j]
                remote(slot, slot, rs2_s.at[q, h, j], rs2_r.at[q, h, j], partner).wait_recv()
            total = ACC[q, x, y, :, cols]
            for j in range(3):
                total = total + U[q, j].astype(jnp.float32)
            OV[rows, cols] = (MV[rows, cols].astype(jnp.float32) - total).astype(jnp.bfloat16)
        pltpu.make_async_copy(OV.at[rows, :], out.at[0, rows, :], out_sem.at[q]).start()

    ag1_start(0)
    for copy in enc_pair():
        copy.start()
    ag1_start(1)
    own_rows(0).start()
    for copy in enc_local():
        copy.start()
    own_rows(1).start()

    def weights(s, carry):
        dec_remote(s).start()
        dec_local(s).start()
        return carry

    lax.fori_loop(0, z + 1, weights, 0)
    mlp_copy.start()

    for h in range(2):
        ag1_wait(0, h)
    own_rows(0).wait()
    for h in range(2):
        ag2_start(0, h)
    ag2_relay(0)
    for h in range(2):
        ag1_wait(1, h)
    own_rows(1).wait()
    for h in range(2):
        ag2_start(1, h)
    ag2_rest(0)
    encode(0)
    z_send(0, 0)
    ag2_relay(1)

    def ready(s, carry):
        dec_arrive(s)
        dec_local(s).wait()
        return carry

    lax.fori_loop(0, z + 1, ready, 0)
    add(0, z, True)
    z_step(0, 0)
    ag2_rest(1)
    encode(1)
    z_send(1, 0)
    add(1, z, True)
    z_step(0, 1)
    z_step(1, 0)
    z_step(0, 2)
    z_step(1, 1)
    z_step(0, 3)
    rs1_start(0)
    z_step(1, 2)
    z_step(1, 3)
    rs1_start(1)
    rs2_start(0)
    finish(0)
    rs2_start(1)
    finish(1)

    for q in range(CHUNKS):
        rows = pl.ds(q * ROWS, ROWS)
        for h in range(2):
            for j in range(3):
                ag1(q, h, j).wait_send()
                rs1(q, h, j).wait_send()
                rs2(q, h, j).wait_send()
            for direction in range(2):
                for piece in range(3):
                    ag2(q, h, direction, piece).wait_send()
        for i in range(FORWARD):
            @pl.when(forward_sends(i))
            def _():
                z_forward(q, i).wait_send()
        for i in range(BACKWARD):
            @pl.when(backward_sends(i))
            def _():
                z_backward(q, i).wait_send()
        pltpu.make_async_copy(OV.at[rows, :], out.at[0, rows, :], out_sem.at[q]).wait()
    for copy in enc_pair():
        copy.wait_send()

    def drained(s, carry):
        dec_remote(s).wait_send()
        return carry

    lax.fori_loop(0, z + 1, drained, 0)


def body(*args):
    bf16, f32 = jnp.bfloat16, jnp.float32
    dma = pltpu.SemaphoreType.DMA
    any_space = pl.BlockSpec(memory_space=pl.ANY)
    block = (CHUNKS, SIDE, SIDE, ROWS, D)
    return pl.pallas_call(
        kernel,
        out_shape=jax.ShapeDtypeStruct(args[0].shape, bf16),
        in_specs=[any_space] * 5,
        out_specs=any_space,
        scratch_shapes=[
            pltpu.VMEM(block, bf16),
            pltpu.VMEM((D, 2 * LANES), bf16),
            pltpu.VMEM((1, 2 * LANES), f32),
            pltpu.VMEM((LAYERS, 2 * LANES, D), bf16),
            pltpu.VMEM((CHUNKS, LAYERS, SIDE * SIDE * ROWS, 2 * LANES), bf16),
            pltpu.VMEM(block, f32),
            pltpu.VMEM(block, bf16),
            pltpu.VMEM((CHUNKS, 3, SIDE, ROWS, HALF), bf16),
            pltpu.VMEM((CHUNKS, 3, SIDE, ROWS, HALF), bf16),
            pltpu.VMEM((CHUNKS, SIDE, ROWS, HALF), bf16),
            pltpu.VMEM((CHUNKS, SIDE, ROWS, HALF), bf16),
            pltpu.VMEM((CHUNKS, 3, ROWS, HALF), bf16),
            pltpu.VMEM((CHUNKS, 3, ROWS, HALF), bf16),
            pltpu.VMEM((CHUNKS * ROWS, D), bf16),
            pltpu.VMEM((CHUNKS * ROWS, D), bf16),
            dma((CHUNKS, 2, 3)), dma((CHUNKS, 2, 3)),
            dma((CHUNKS, 2, 2, 3)), dma((CHUNKS, 2, 2, 3)),
            dma((2,)), dma((2,)),
            dma((LAYERS,)), dma((LAYERS,)),
            dma((CHUNKS, FORWARD)), dma((CHUNKS, FORWARD)),
            dma((CHUNKS, BACKWARD)), dma((CHUNKS, BACKWARD)),
            dma((CHUNKS, 2, 3)), dma((CHUNKS, 2, 3)),
            dma((CHUNKS, 2, 3)), dma((CHUNKS, 2, 3)),
            dma((CHUNKS,)), dma((3,)), dma((LAYERS,)), dma((CHUNKS,)),
        ],
        compiler_params=pltpu.CompilerParams(
            collective_id=0, has_side_effects=True, vmem_limit_bytes=60 * 2**20
        ),
    )(*args)


def solution(mesh):
    return jax.shard_map(
        body,
        mesh=mesh,
        in_specs=(
            P("layer", "latent", None),
            P("layer", "latent", None),
            P("layer", None, "latent"),
            P("layer", "latent"),
            P("layer", None, "latent", None),
        ),
        out_specs=P("layer", "latent", None),
        check_vma=False,
    )
```

time: 356 us -> 84.7 us (0.24)
  waiting for transfers between devices: 223 us -> 0 us
  matrix products: 116 us -> 0 us
  Pallas kernels: 0 us -> 82.9 us
  between operations: 13.1 us -> 0.01 us
    reduce_scatter x1 -> x0, waiting for transfers between devices: 122 us -> none  [body(): mine = lax.psum_scatter(recon, 'latent', scatter_dimension=0, tiled=True)]
    dot_general x9 -> x0, matrix products: 116 us -> none  [the longest x8 109 us: added(): return value + jnp.dot(block, chosen, preferred_element_type=jnp.float32)]
    all_gather x2 -> x0, waiting for transfers between devices: 100 us -> none  [the longest x1 60.8 us: body(): lax.all_gather(resid[0], 'latent', axis=0, tiled=True)]
    pallas_call x0 -> x1, Pallas kernels: none -> 82.9 us  [body(): pl.pallas_call(kernel, out_shape=jax.ShapeDtypeStruct(args[0].shape, bf16...]
  transfers between devices with their start and end apart: 3 -> 0, of which waited for: 3 -> 0; matrix products, arithmetic and copies ran while one was open for 0% -> 0% of each run, Pallas kernels for 0% -> 0%
where the time goes in v1:
time: 84.7 us; the launch traced here: 84.6 us
  Pallas kernels  82.9 us (98%)
  local copies, waits for them, and re-layouts  1.67 us (2%)
    pallas_call x1, Pallas kernels, body(): pl.pallas_call(kernel, out_shape=jax.ShapeDtypeStruct(args[0].shape, bf16...  82.9 us

profile of v1, /device:TPU:224, one launch (start us, length us, event | category | flops | bytes accessed | tf_op | source)
XLA Modules:
  0.0 84.6 jit_solution(15704724257951675481)
XLA Ops:
  0.0 82.9 %shard_map.55 = bf16[1,32,4096]{2,1,0:T(8,128)(2,1)} custom-call(bf16[1,32,4096]{2,1,0:T(8,128)(2,1)} %resid.1, bf16[1,32,4096]{2,1,0:T(8,128)(2,1)} %mlp.1, bf16[1,4096,128]{2,1,0:T(8,128)(2,1)} %enc.1, f32[1,128]{1,0:T(1,128)} %bias.1, bf16[1,8,128,4096]{3,2,1,0:T(8,128)(2,1)} %dec.1), custom_call_target="tpu_custom_call" | custom-call | tf_op jit(solution)/shard_map/pallas_call | solution.py:382
  82.9 1.7 %copy.7 = bf16[1,32,4096]{2,1,0:T(8,128)(2,1)} copy(bf16[1,32,4096]{2,1,0:T(8,128)(2,1)} %shard_map.55) | data formatting | bytes 524288

commit v2 on v1

--- a/solution.py
+++ b/solution.py
@@ -10,23 +10,35 @@
 MESH = pl.DeviceIdType.MESH
 LAYERS = 8
 SIDE = 4
-CHUNKS = 2
-ROWS = 16
+CHUNKS = 4
+ROWS = 8
 D = 4096
 HALF = 2048
 QUARTER = 1024
 LANES = 128
-TILE = 512
+TILE = 2048
 OFFSETS = (1, SIDE - 1, 2)
 FORWARD = 4
 BACKWARD = 3
 
+SCHEDULE = (
+    ("first", 0), ("start", 0), ("first", 1), ("first", 2), ("first", 3), ("second", 0),
+    ("second", 1), ("relay", 0), ("second", 2), ("relay", 1), ("second", 3),
+    ("code", 0), ("send", 0), ("relay", 2), ("own", 0), ("z0", 0), ("code", 1),
+    ("send", 1), ("relay", 3), ("own", 1), ("z1", 0), ("z0", 1), ("code", 2), ("z2", 0),
+    ("send", 2), ("own", 2), ("z1", 1), ("code", 3), ("own", 3), ("z3", 0), ("rs1", 0),
+    ("z0", 2), ("z2", 1), ("send", 3), ("z1", 2), ("add", 0), ("z3", 1), ("rs1", 1),
+    ("z0", 3), ("z2", 2), ("rs2", 0), ("z1", 3), ("add", 1), ("z3", 2), ("rs1", 2),
+    ("end", 0), ("z2", 3), ("rs2", 1), ("add", 2), ("z3", 3), ("rs1", 3), ("end", 1),
+    ("rs2", 2), ("add", 3), ("end", 2), ("rs2", 3), ("end", 3),
+)
+
 
 def kernel(
     resid, mlp, enc, bias, dec, out,
-    R, WE, BE, WD, L, ACC, S, TA, TB, VA, VB, UA, UB, MV, OV,
+    R, WE, BE, WD, L, ACC, S, FA, FB, TA, TB, VA, VB, UA, UB, MV, OV,
     ag1_s, ag1_r, ag2_s, ag2_r, w_s, w_r, d_s, d_r, zf_s, zf_r, zb_s, zb_r,
-    rs1_s, rs1_r, rs2_s, rs2_r, own_sem, loc_sem, dloc_sem, out_sem,
+    rs1_s, rs1_r, rs2_s, rs2_r, own_sem, mlp_sem, loc_sem, dloc_sem, out_sem,
 ):
     z = lax.axis_index("layer")
     index = lax.axis_index("latent")
@@ -149,7 +161,8 @@
     def own_rows(q):
         return pltpu.make_async_copy(resid.at[0, pl.ds(q * ROWS, ROWS), :], R.at[q, x, y], own_sem.at[q])
 
-    mlp_copy = pltpu.make_async_copy(mlp.at[0], MV, loc_sem.at[2])
+    def mlp_copy(q):
+        return pltpu.make_async_copy(mlp.at[0, pl.ds(q * ROWS, ROWS), :], MV.at[q], mlp_sem.at[q])
 
     def encode(q):
         if q == 0:
@@ -198,6 +211,10 @@
                 remote(slot, slot, zb_s.at[q, i], zb_r.at[q, i], partner).wait_recv()
 
     def add(q, s, first):
+        if q == 0:
+            dec_arrive(s)
+            dec_local(s).wait()
+
         def tile(n, carry):
             cols = pl.ds(pl.multiple_of(n * TILE, TILE), TILE)
             part = jnp.dot(L[q, s], WD[s, :, cols], preferred_element_type=jnp.float32)
@@ -227,12 +244,27 @@
         z_send(q, i + 1)
         z_add(q, i)
 
-    def rs1(q, h, j):
-        cols = pl.ds(h * HALF, HALF)
-        o = OFFSETS[j]
-        if h == 0:
-            return remote(S.at[q, move(x, o), :, :, cols], TA.at[q, j], rs1_s.at[q, h, j], rs1_r.at[q, h, j], at_chip(move(x, o), y))
-        return remote(S.at[q, :, move(y, o), :, cols], TB.at[q, j], rs1_s.at[q, h, j], rs1_r.at[q, h, j], at_chip(x, move(y, o)))
+    def line_of(h, offset):
+        return move(x, offset) if h == 0 else move(y, offset)
+
+    def place(q, h, k, cols):
+        return (q, k, slice(None), slice(None), cols) if h == 0 else (q, slice(None), k, slice(None), cols)
+
+    def neighbour(h, offset):
+        return at_chip(move(x, offset), y) if h == 0 else at_chip(x, move(y, offset))
+
+    def rs1(q, h, direction, piece):
+        step = 1 if direction == 0 else SIDE - 1
+        quarter = direction if piece != 1 else 1 - direction
+        cols = pl.ds(h * HALF + quarter * QUARTER, QUARTER)
+        src = S.at[place(q, h, line_of(h, 2 if piece == 0 else step), cols)]
+        dst = (FA, FB)[h].at[q, direction] if piece == 0 else (TA, TB)[h].at[q, direction, :, :, pl.ds(quarter * QUARTER, QUARTER)]
+        return remote(src, dst, rs1_s.at[q, h, direction, piece], rs1_r.at[q, h, direction, piece], neighbour(h, step))
+
+    def rs1_arrive(q, h, direction, piece):
+        quarter = direction if piece != 1 else 1 - direction
+        slot = (FA, FB)[h].at[q, direction] if piece == 0 else (TA, TB)[h].at[q, direction, :, :, pl.ds(quarter * QUARTER, QUARTER)]
+        remote(slot, slot, rs1_s.at[q, h, direction, piece], rs1_r.at[q, h, direction, piece], partner).wait_recv()
 
     def rs1_start(q):
         def tile(n, carry):
@@ -241,9 +273,20 @@
             return carry
 
         lax.fori_loop(0, D // TILE, tile, 0)
-        for j in (2, 0, 1):
+        for piece in range(2):
             for h in range(2):
-                rs1(q, h, j).start()
+                for direction in range(2):
+                    rs1(q, h, direction, piece).start()
+
+    def rs1_relay(q):
+        for h in range(2):
+            for direction in range(2):
+                step = 1 if direction == 0 else SIDE - 1
+                rs1_arrive(q, h, direction, 0)
+                at = place(q, h, line_of(h, step), pl.ds(h * HALF + direction * QUARTER, QUARTER))
+                far = (FA, FB)[h][q, direction].astype(jnp.float32)
+                S[at] = (ACC[at] + far).astype(jnp.bfloat16)
+                rs1(q, h, direction, 2).start()
 
     def rs2(q, h, j):
         o = OFFSETS[j]
@@ -254,14 +297,14 @@
     def rs2_start(q):
         for h, T, V in ((0, TA, VA), (1, TB, VB)):
             cols = pl.ds(h * HALF, HALF)
-            for j in (0, 1, 2):
-                slot = T.at[q, j]
-                remote(slot, slot, rs1_s.at[q, h, j], rs1_r.at[q, h, j], partner).wait_recv()
+            for piece in (1, 2):
+                for direction in range(2):
+                    rs1_arrive(q, h, direction, piece)
 
             def line(k, carry):
                 at = (q, x, k, slice(None), cols) if h == 0 else (q, k, y, slice(None), cols)
                 total = ACC[at]
-                for j in range(3):
+                for j in range(2):
                     total = total + T[q, j, k].astype(jnp.float32)
                 ACC[at] = total
                 V[q, k] = total.astype(jnp.bfloat16)
@@ -271,10 +314,11 @@
             for j in (2, 0, 1):
                 rs2(q, h, j).start()
 
+    def result(q):
+        return pltpu.make_async_copy(OV.at[q], out.at[0, pl.ds(q * ROWS, ROWS), :], out_sem.at[q])
+
     def finish(q):
-        if q == 0:
-            mlp_copy.wait()
-        rows = pl.ds(q * ROWS, ROWS)
+        mlp_copy(q).wait()
         for h, U in ((0, UA), (1, UB)):
             cols = pl.ds(h * HALF, HALF)
             for j in (0, 1, 2):
@@ -283,78 +327,61 @@
             total = ACC[q, x, y, :, cols]
             for j in range(3):
                 total = total + U[q, j].astype(jnp.float32)
-            OV[rows, cols] = (MV[rows, cols].astype(jnp.float32) - total).astype(jnp.bfloat16)
-        pltpu.make_async_copy(OV.at[rows, :], out.at[0, rows, :], out_sem.at[q]).start()
-
-    ag1_start(0)
-    for copy in enc_pair():
-        copy.start()
-    ag1_start(1)
-    own_rows(0).start()
-    for copy in enc_local():
-        copy.start()
-    own_rows(1).start()
-
-    def weights(s, carry):
-        dec_remote(s).start()
-        dec_local(s).start()
+            OV[q, :, cols] = (MV[q, :, cols].astype(jnp.float32) - total).astype(jnp.bfloat16)
+        result(q).start()
+
+    def weights(k, carry):
+        dec_remote(z - k).start()
+        dec_local(z - k).start()
         return carry
 
-    lax.fori_loop(0, z + 1, weights, 0)
-    mlp_copy.start()
-
-    for h in range(2):
-        ag1_wait(0, h)
-    own_rows(0).wait()
-    for h in range(2):
-        ag2_start(0, h)
-    ag2_relay(0)
-    for h in range(2):
-        ag1_wait(1, h)
-    own_rows(1).wait()
-    for h in range(2):
-        ag2_start(1, h)
-    ag2_rest(0)
-    encode(0)
-    z_send(0, 0)
-    ag2_relay(1)
-
-    def ready(s, carry):
-        dec_arrive(s)
-        dec_local(s).wait()
-        return carry
-
-    lax.fori_loop(0, z + 1, ready, 0)
-    add(0, z, True)
-    z_step(0, 0)
-    ag2_rest(1)
-    encode(1)
-    z_send(1, 0)
-    add(1, z, True)
-    z_step(0, 1)
-    z_step(1, 0)
-    z_step(0, 2)
-    z_step(1, 1)
-    z_step(0, 3)
-    rs1_start(0)
-    z_step(1, 2)
-    z_step(1, 3)
-    rs1_start(1)
-    rs2_start(0)
-    finish(0)
-    rs2_start(1)
-    finish(1)
+    def start(q):
+        for copy in enc_pair():
+            copy.start()
+        for copy in enc_local():
+            copy.start()
+        for c in range(CHUNKS):
+            own_rows(c).start()
+        lax.fori_loop(0, z + 1, weights, 0)
+        for c in range(CHUNKS):
+            mlp_copy(c).start()
+
+    def second(q):
+        own_rows(q).wait()
+        for h in range(2):
+            ag1_wait(q, h)
+        for h in range(2):
+            ag2_start(q, h)
+
+    def code(q):
+        ag2_rest(q)
+        encode(q)
+
+    def send(q):
+        z_send(q, 0)
+
+    def own(q):
+        add(q, z, True)
+
+    steps = {
+        "first": ag1_start, "start": start, "second": second, "relay": ag2_relay,
+        "code": code, "send": send, "own": own, "rs1": rs1_start, "add": rs1_relay, "rs2": rs2_start, "end": finish,
+    }
+    for name, q in SCHEDULE:
+        if name[0] == "z":
+            z_step(q, int(name[1]))
+        else:
+            steps[name](q)
 
     for q in range(CHUNKS):
-        rows = pl.ds(q * ROWS, ROWS)
         for h in range(2):
             for j in range(3):
                 ag1(q, h, j).wait_send()
-                rs1(q, h, j).wait_send()
                 rs2(q, h, j).wait_send()
             for direction in range(2):
                 for piece in range(3):
                     ag2(q, h, direction, piece).wait_send()
+                    rs1(q, h, direction, piece).wait_send()
         for i in range(FORWARD):
             @pl.when(forward_sends(i))
             def _():
@@ -363,7 +390,7 @@
             @pl.when(backward_sends(i))
             def _():
                 z_backward(q, i).wait_send()
-        pltpu.make_async_copy(OV.at[rows, :], out.at[0, rows, :], out_sem.at[q]).wait()
+        result(q).wait()
     for copy in enc_pair():
         copy.wait_send()
 
@@ -392,23 +419,25 @@
             pltpu.VMEM((CHUNKS, LAYERS, SIDE * SIDE * ROWS, 2 * LANES), bf16),
             pltpu.VMEM(block, f32),
             pltpu.VMEM(block, bf16),
-            pltpu.VMEM((CHUNKS, 3, SIDE, ROWS, HALF), bf16),
-            pltpu.VMEM((CHUNKS, 3, SIDE, ROWS, HALF), bf16),
+            pltpu.VMEM((CHUNKS, 2, SIDE, ROWS, QUARTER), bf16),
+            pltpu.VMEM((CHUNKS, 2, SIDE, ROWS, QUARTER), bf16),
+            pltpu.VMEM((CHUNKS, 2, SIDE, ROWS, HALF), bf16),
+            pltpu.VMEM((CHUNKS, 2, SIDE, ROWS, HALF), bf16),
             pltpu.VMEM((CHUNKS, SIDE, ROWS, HALF), bf16),
             pltpu.VMEM((CHUNKS, SIDE, ROWS, HALF), bf16),
             pltpu.VMEM((CHUNKS, 3, ROWS, HALF), bf16),
             pltpu.VMEM((CHUNKS, 3, ROWS, HALF), bf16),
-            pltpu.VMEM((CHUNKS * ROWS, D), bf16),
-            pltpu.VMEM((CHUNKS * ROWS, D), bf16),
+            pltpu.VMEM((CHUNKS, ROWS, D), bf16),
+            pltpu.VMEM((CHUNKS, ROWS, D), bf16),
             dma((CHUNKS, 2, 3)), dma((CHUNKS, 2, 3)),
             dma((CHUNKS, 2, 2, 3)), dma((CHUNKS, 2, 2, 3)),
             dma((2,)), dma((2,)),
             dma((LAYERS,)), dma((LAYERS,)),
             dma((CHUNKS, FORWARD)), dma((CHUNKS, FORWARD)),
             dma((CHUNKS, BACKWARD)), dma((CHUNKS, BACKWARD)),
+            dma((CHUNKS, 2, 2, 3)), dma((CHUNKS, 2, 2, 3)),
             dma((CHUNKS, 2, 3)), dma((CHUNKS, 2, 3)),
-            dma((CHUNKS, 2, 3)), dma((CHUNKS, 2, 3)),
-            dma((CHUNKS,)), dma((3,)), dma((LAYERS,)), dma((CHUNKS,)),
+            dma((CHUNKS,)), dma((CHUNKS,)), dma((2,)), dma((LAYERS,)), dma((CHUNKS,)),
         ],
         compiler_params=pltpu.CompilerParams(
             collective_id=0, has_side_effects=True, vmem_limit_bytes=60 * 2**20

time: 84.7 us -> 72.3 us (0.85)
  Pallas kernels: 82.9 us -> 70.5 us
    pallas_call x1, Pallas kernels: 82.9 us -> 70.5 us  [body(): pl.pallas_call(kernel, out_shape=jax.ShapeDtypeStruct(args[0].shape, bf16...]
where the time goes in v2:
time: 72.3 us; the launch traced here: 72.2 us
  Pallas kernels  70.5 us (98%)
  local copies, waits for them, and re-layouts  1.67 us (2%)
    pallas_call x1, Pallas kernels, body(): pl.pallas_call(kernel, out_shape=jax.ShapeDtypeStruct(args[0].shape, bf16...  70.5 us
    unnamed x1, local copies, waits for them, and re-layouts  1.67 us

profile of v2, /device:TPU:224, one launch (start us, length us, event | category | flops | bytes accessed | tf_op | source)
XLA Modules:
  0.0 72.2 jit_solution(7640554032012840322)
XLA Ops:
  0.0 70.5 %shard_map.55 = bf16[1,32,4096]{2,1,0:T(8,128)(2,1)} custom-call(bf16[1,32,4096]{2,1,0:T(8,128)(2,1)} %resid.1, bf16[1,32,4096]{2,1,0:T(8,128)(2,1)} %mlp.1, bf16[1,4096,128]{2,1,0:T(8,128)(2,1)} %enc.1, f32[1,128]{1,0:T(1,128)} %bias.1, bf16[1,8,128,4096]{3,2,1,0:T(8,128)(2,1)} %dec.1), custom_call_target="tpu_custom_call" | custom-call | tf_op jit(solution)/shard_map/pallas_call | solution.py:409
  70.6 1.7 %copy.7 = bf16[1,32,4096]{2,1,0:T(8,128)(2,1)} copy(bf16[1,32,4096]{2,1,0:T(8,128)(2,1)} %shard_map.55) | data formatting | bytes 524288

commit v3 on v2

--- a/solution.py
+++ b/solution.py
@@ -16,7 +16,7 @@
 HALF = 2048
 QUARTER = 1024
 LANES = 128
-TILE = 2048
+TILE = 4096
 OFFSETS = (1, SIDE - 1, 2)
 FORWARD = 4
 BACKWARD = 3
@@ -83,7 +83,7 @@
         )
 
     def ag1_start(q):
-        for j in range(3):
+        for j in (2, 0, 1):
             for h in range(2):
                 ag1(q, h, j).start()
 

time: 72.3 us -> 72 us (level)
  no operation moved by 1% of the time
where the time goes in v3:
time: 72 us; the launch traced here: 71.9 us
  Pallas kernels  70.2 us (98%)
  local copies, waits for them, and re-layouts  1.67 us (2%)
    pallas_call x1, Pallas kernels, body(): pl.pallas_call(kernel, out_shape=jax.ShapeDtypeStruct(args[0].shape, bf16...  70.2 us
    unnamed x1, local copies, waits for them, and re-layouts  1.67 us

profile of v3, /device:TPU:224, one launch (start us, length us, event | category | flops | bytes accessed | tf_op | source)
XLA Modules:
  0.0 71.9 jit_solution(12971497852507941229)
XLA Ops:
  0.0 70.2 %shard_map.55 = bf16[1,32,4096]{2,1,0:T(8,128)(2,1)} custom-call(bf16[1,32,4096]{2,1,0:T(8,128)(2,1)} %resid.1, bf16[1,32,4096]{2,1,0:T(8,128)(2,1)} %mlp.1, bf16[1,4096,128]{2,1,0:T(8,128)(2,1)} %enc.1, f32[1,128]{1,0:T(1,128)} %bias.1, bf16[1,8,128,4096]{3,2,1,0:T(8,128)(2,1)} %dec.1), custom_call_target="tpu_custom_call" | custom-call | tf_op jit(solution)/shard_map/pallas_call | solution.py:409
  70.2 1.7 %copy.7 = bf16[1,32,4096]{2,1,0:T(8,128)(2,1)} copy(bf16[1,32,4096]{2,1,0:T(8,128)(2,1)} %shard_map.55) | data formatting | bytes 524288
